TPU v7x, 256 devices: a whole 4x4x8 slice. The times are simulated.
256 devices in a mesh: bag: 64 (over y, z, core), seq: 4 (over x).
Axes of the slice: x: 4, y: 4, z: 8, core: 2. Of those that a mesh axis runs over, the one named last changes fastest.
Arguments:
- video: bfloat16 [32768, 5120], P('bag'), may hold values from -6 to 6
- w_query: bfloat16 [5120, 5120], P('bag', 'seq'), may hold values from -0.078125 to 0.078125
- cond_kv: bfloat16 [64, 512, 2, 5120], P('bag', None, None, 'seq'), may hold values from -400 to 400, as said below
- neg_kv: bfloat16 [512, 2, 5120], P('bag', None, 'seq'), may hold values from -400 to 400, as said below
- prompt_len: int32 [64], P('bag'), may hold values from 1 to 512
- neg_len: int32 [1], replicated, may hold values from 1 to 512
Outputs:
- guided: bfloat16 [32768, 5120], P('bag', 'seq')
Inputs may be any that keep to these rules, and one draw needn't show every extreme that they name: `cond_kv`: finite keys and values. `neg_kv`: finite keys and values.
All inputs are finite; a program needn't handle non-finite values.
Results may differ from a plain program's by a relative error of at most 0.012.
The roundings to bfloat16 on the way count: a program that leaves them out, or rounds other values in their place, can miss the bound.
Values may be sent and summed in bfloat16 or wider, within the bound.
No kernel may reach another device: no remote copies, remote signals or barrier semaphores. Data moves between devices by JAX's collectives and lax.ppermute only.
A program may use at most 128 MiB of HBM per device.

v0:
```python
import jax
import jax.numpy as jnp
from jax import lax
from jax.sharding import PartitionSpec as P

DM = 5120
HD = 128
guidance_scale = 5.0


def layer_norm(video):
    values = video.astype(jnp.float32)
    center = values - jnp.mean(values, axis=-1, keepdims=True)
    spread = jnp.mean(center * center, axis=-1, keepdims=True)
    return (center * lax.rsqrt(spread + 1e-06)).astype(jnp.bfloat16)


def negative_rows(neg_kv):
    return lax.all_gather(neg_kv, "bag", axis=0, tiled=True)


def attend(query_rms, keys, values, length):
    tok_rows = query_rms.shape[0]
    key_rows = keys.shape[0]
    local_heads = query_rms.shape[1] // HD
    q_heads = query_rms.reshape(tok_rows, local_heads, HD)
    k_heads = keys.reshape(key_rows, local_heads, HD)
    v_heads = values.reshape(key_rows, local_heads, HD)
    scores = jnp.einsum(
        "thd,shd->hts", q_heads, k_heads, preferred_element_type=jnp.float32
    ) / jnp.sqrt(jnp.float32(HD))
    live = (jnp.arange(key_rows, dtype=jnp.int32) < length)[None, None, :]
    scores = jnp.where(live, scores, jnp.float32(-1e30))
    top = jnp.max(scores, axis=-1, keepdims=True)
    weights = jnp.where(live, jnp.exp(scores - top), jnp.float32(0.0))
    weights = (weights / jnp.sum(weights, axis=-1, keepdims=True)).astype(jnp.bfloat16)
    mixed = jnp.einsum("hts,shd->thd", weights, v_heads, preferred_element_type=jnp.float32)
    return mixed.reshape(tok_rows, local_heads * HD)


def body(video, w_query, cond_kv, neg_kv, prompt_len, neg_len):
    normed = layer_norm(video)
    gathered = lax.all_gather(w_query, "bag", axis=0, tiled=True)
    query = jnp.dot(normed, gathered, preferred_element_type=jnp.float32)
    squares = lax.psum(jnp.sum(query * query, axis=1), "seq")
    query_rms = (query * lax.rsqrt(squares / DM + 1e-06)[:, None]).astype(jnp.bfloat16)
    negative = negative_rows(neg_kv)
    cond = attend(query_rms, cond_kv[0, :, 0], cond_kv[0, :, 1], prompt_len[0])
    uncond = attend(query_rms, negative[:, 0], negative[:, 1], neg_len[0])
    return (uncond + guidance_scale * (cond - uncond)).astype(jnp.bfloat16)


def solution(mesh):
    in_specs = (
        P("bag", None),
        P("bag", "seq"),
        P("bag", None, None, "seq"),
        P("bag", None, "seq"),
        P("bag"),
        P(),
    )
    out_specs = P("bag", "seq")
    return jax.shard_map(body, mesh=mesh, in_specs=in_specs, out_specs=out_specs, check_vma=False)
```

profile of v0, /device:TPU:32, one launch (start us, length us, event | category | flops | bytes accessed | tf_op | source)
XLA Modules:
  0.0 257.8 jit_solution(1056586922885122837)
XLA Ops:
  6.5 0.0 all-gather.5.cloned.1.call-start
  6.5 0.7 all-gather.5.cloned.1.call-update
  7.3 0.0 all-gather.3.cloned.1.call-start
  7.3 0.7 all-gather.3.cloned.1.call-update
  9.3 7.7 %fusion.28 = (bf16[1,512,1,1280]{3,2,1,0:T(2,128)(2,1)}, bf16[1,512,1,1280]{3,2,1,0:T(2,128)(2,1)S(1)}) fusion(bf16[1,512,2,1280]{3,2,1,0:T(2,128)(2,1)} %param.8), kind=kLoop, calls=%fused_computation.41 | loop fusion | bytes 5242880 | tf_op jit(solution)/shard_map/slice | solution.py:48
  17.0 6.2 %copy.50 = bf16[1,512,1,1280]{1,3,2,0:T(8,128)(2,1)} copy(bf16[1,512,1,1280]{3,2,1,0:T(2,128)(2,1)} %get-tuple-element.5) | data formatting | bytes 2621440
  23.1 3.8 %copy.38 = bf16[1,512,1,1280]{1,3,2,0:T(8,128)(2,1)} copy(bf16[1,512,1,1280]{3,2,1,0:T(2,128)(2,1)S(1)} %get-tuple-element.6) | data formatting | bytes 2621440 | tf_op jit(solution)/shard_map/slice | solution.py:48
  27.0 3.3 %convert_reduce_fusion = f32[512]{0:T(512)S(1)} fusion(bf16[512,5120]{1,0:T(8,128)(2,1)} %param.6), kind=kLoop, calls=%fused_computation.3 | loop fusion | flops 5242368 | bytes 5244928 | tf_op jit(solution)/shard_map/reduce_sum | solution.py:13
  30.2 4.0 %fusion.4 = f32[512]{0:T(512)S(1)} fusion(bf16[512,5120]{1,0:T(8,128)(2,1)} %param.6, f32[512]{0:T(512)S(1)} %broadcast_multiply_fusion), kind=kLoop, calls=%fused_computation.6 | loop fusion | flops 10485248 | bytes 5246976 | tf_op jit(solution)/shard_map/reduce_sum | solution.py:14
  34.2 55.3 %all-gather.5.cloned.1.call-done = bf16[512,2,1280]{2,1,0:T(2,128)(2,1)} async-done(((bf16[8,2,1280]{2,1,0:T(2,128)(2,1)}), bf16[512,2,1280]{2,1,0:T(2,128)(2,1)}) %all-gather.5.cloned.1.call-update) | async-done | bytes 2621456 | tf_op jit(solution)/shard_map/all_gather | solution.py:19
  89.5 7.7 %fusion.29 = (bf16[512,1,1280]{2,1,0:T(2,128)(2,1)}, bf16[512,1,1280]{2,1,0:T(2,128)(2,1)S(1)}) fusion(bf16[512,2,1280]{2,1,0:T(2,128)(2,1)} %all-gather.5.cloned.1.call-done), kind=kLoop, calls=%fused_computation.42 | loop fusion | bytes 5242880 | tf_op jit(solution)/shard_map/slice | solution.py:49
  97.2 6.2 %copy.49 = bf16[512,1,1280]{0,2,1:T(8,128)(2,1)} copy(bf16[512,1,1280]{2,1,0:T(2,128)(2,1)} %get-tuple-element.7) | data formatting | bytes 2621440
  103.4 3.7 %copy.33 = bf16[512,1,1280]{0,2,1:T(8,128)(2,1)} copy(bf16[512,1,1280]{2,1,0:T(2,128)(2,1)S(1)} %get-tuple-element.8) | data formatting | bytes 2621440 | tf_op jit(solution)/shard_map/slice | solution.py:49
  107.1 74.0 %all-gather.3.cloned.1.call-done = bf16[5120,1280]{1,0:T(8,128)(2,1)} async-done(((bf16[80,1280]{1,0:T(8,128)(2,1)}), bf16[5120,1280]{1,0:T(8,128)(2,1)}) %all-gather.3.cloned.1.call-update) | async-done | bytes 13107216 | tf_op jit(solution)/shard_map/all_gather | solution.py:43
  181.2 14.0 %multiply_reduce_fusion = (f32[512]{0:T(512)S(1)}, f32[512,1280]{1,0:T(8,128)}) fusion(bf16[5120,1280]{1,0:T(8,128)(2,1)} %all-gather.3.cloned.1.call-done, bf16[512,5120]{1,0:T(8,128)(2,1)} %param.6, f32[512]{0:T(512)S(1)} %add_rsqrt_fusion.1, f32[512]{0:T(512)S(1)} %broadcast_multiply_fusion), kind=kOutput, calls=%fused_computation.29 | convolution fusion | flops 6722682368 | bytes 20977664 | tf_op jit(solution)/shard_map/dot_general | solution.py:44
  195.1 10.6 %psum.7 = f32[512]{0:T(512)S(1)} all-reduce(f32[512]{0:T(512)S(1)} %get-tuple-element.9), channel_id=1, replica_groups=mesh['bag'=64,'seq'=4] {'seq'}, use_global_device_ids=true, to_apply=%region_3.0 | all-reduce | flops 512 | bytes 4096 | tf_op jit(solution)/shard_map/psum | solution.py:45
  205.7 1.9 multiply_convert_fusion
  207.7 0.7 copy.29
  208.3 0.0 copy-start
  208.3 0.0 copy-start.1
  208.4 10.5 %fusion.31 = (f32[10,512]{1,0:T(8,128)S(1)}, f32[10,512,512]{1,2,0:T(8,128)}) fusion(pred[512]{0:T(512)(128)(4,1)S(1)} %iota_compare_fusion, bf16[512,10,128]{0,2,1:T(8,128)(2,1)S(1)} %bitcast.28, bf16[512,10,128]{0,2,1:T(8,128)(2,1)} %bitcast.31), kind=kOutput, calls=%fused_computation.44 | convolution fusion | flops 684196352 | bytes 13128192 | tf_op jit(solution)/shard_map/sub | solution.py:35
  218.9 0.0 copy-done
  218.9 0.0 copy-done.1
  218.9 6.4 %fusion.19 = f32[10,512,128]{1,2,0:T(8,128)} fusion(bf16[512,10,128]{0,2,1:T(8,128)(2,1)S(1)} %bitcast.30, f32[10,512,512]{1,2,0:T(8,128)} %get-tuple-element.14, f32[10,512]{1,0:T(8,128)S(1)} %get-tuple-element.13), kind=kOutput, calls=%fused_computation.26 | convolution fusion | flops 676331520 | bytes 14438400 | tf_op jit(solution)/shard_map/hts,shd->thd/dot_general | solution.py:37
  225.2 2.1 copy.40
  227.4 10.4 %fusion.30 = (f32[10,512]{1,0:T(8,128)S(1)}, f32[10,512,512]{1,2,0:T(8,128)}) fusion(pred[512]{0:T(512)(128)(4,1)S(1)} %iota_compare_fusion.1, bf16[512,10,128]{0,2,1:T(8,128)(2,1)} %bitcast.29, bf16[512,10,128]{0,2,1:T(8,128)(2,1)} %bitcast.33), kind=kOutput, calls=%fused_computation.43 | convolution fusion | flops 684196352 | bytes 13128192 | tf_op jit(solution)/shard_map/sub | solution.py:35
  237.8 6.8 %fusion.18 = f32[10,512,128]{1,2,0:T(8,128)} fusion(bf16[512,10,128]{0,2,1:T(8,128)(2,1)} %bitcast.32, f32[10,512,512]{1,2,0:T(8,128)} %get-tuple-element.12, f32[10,512]{1,0:T(8,128)S(1)} %get-tuple-element.11), kind=kOutput, calls=%fused_computation.25 | convolution fusion | flops 676331520 | bytes 14438400 | tf_op jit(solution)/shard_map/hts,shd->thd/dot_general | solution.py:37
  244.6 3.2 %copy.42 = f32[512,1280]{1,0:T(8,128)} copy(f32[512,1280]{0,1:T(8,128)} %bitcast.27) | data formatting | bytes 5242880 | tf_op jit(solution)/shard_map/reshape | solution.py:38
  247.8 3.1 %add_convert_fusion = bf16[512,1280]{1,0:T(8,128)(2,1)} fusion(f32[512,1280]{1,0:T(8,128)} %copy.42, f32[512,1280]{1,0:T(8,128)S(1)} %copy.40), kind=kLoop, calls=%fused_computation.27 | loop fusion | flops 2621440 | bytes 6553600 | tf_op jit(solution)/shard_map/convert_element_type | solution.py:50
  (5 shorter events, 0.0 us)
Async XLA Ops:
  6.5 83.0 %all-gather.5.cloned.1.call-start = ((), (), s32[]{:S(2)}) async-start(), calls=%async_computation.1 | async-start | bytes 2662400 | tf_op jit(solution)/shard_map/all_gather | solution.py:19
  7.3 173.9 %all-gather.3.cloned.1.call-start = ((), (), s32[]{:S(2)}) async-start(), calls=%async_computation | async-start | bytes 13312000 | tf_op jit(solution)/shard_map/all_gather | solution.py:43
  208.3 10.5 %copy-start = (bf16[512,1280]{0,1:T(8,128)(2,1)}, bf16[512,1280]{0,1:T(8,128)(2,1)S(1)}, u32[]{:S(2)}) copy-start(bf16[512,1280]{0,1:T(8,128)(2,1)S(1)} %copy.29) | copy-start | bytes 3932164
  208.3 10.5 %copy-start.1 = (bf16[1,512,1,1280]{1,3,2,0:T(8,128)(2,1)S(1)}, bf16[1,512,1,1280]{1,3,2,0:T(8,128)(2,1)}, u32[]{:S(2)}) copy-start(bf16[1,512,1,1280]{1,3,2,0:T(8,128)(2,1)} %copy.38) | copy-start | bytes 3932164
Sparse Core Ops, SparseCore 0:
  10.1 79.3 all-gather.4
  92.3 88.8 all-gather.2
where the time goes:
time: 259 us; the launch traced here: 258 us
  waiting for transfers between devices  131 us (51%)
  matrix products  48 us (19%)
  local copies, waits for them, and re-layouts  41.3 us (16%)
  between operations  14.7 us (6%)
  other arithmetic  12.4 us (5%)
  blocking collectives  10.6 us (4%)
    all_gather x1, waiting for transfers between devices, body(): gathered = lax.all_gather(w_query, 'bag', axis=0, tiled=True)  74 us
    all_gather x1, waiting for transfers between devices, negative_rows(): return lax.all_gather(neg_kv, 'bag', axis=0, tiled=True)  55.3 us
    sub x2, matrix products, attend(): weights = jnp.where(live, jnp.exp(scores - top), jnp.float32(0.0))  20.9 us
    dot_general x1, matrix products, body(): query = jnp.dot(normed, gathered, preferred_element_type=jnp.float32)  14 us
    dot_general x2, matrix products, attend(): jnp.einsum('hts,shd->thd', weights, v_heads, preferred_element_type=jnp.f...  13.1 us
    unnamed x6, local copies, waits for them, and re-layouts  12.4 us
    slice x2, local copies, waits for them, and re-layouts, body(): cond = attend(query_rms, cond_kv[0, :, 0], cond_kv[0, :, 1], prompt_len[0])  11.5 us
    slice x2, local copies, waits for them, and re-layouts, body(): uncond = attend(query_rms, negative[:, 0], negative[:, 1], neg_len[0])  11.4 us
  transfers between devices with their start and end apart: 2, of which 2 were waited for; matrix products, arithmetic and copies ran while one was open for 17% of the time, Pallas kernels for 0%

commit v1 on v0

--- a/solution.py
+++ b/solution.py
@@ -8,6 +8,13 @@
 guidance_scale = 5.0
 
 
+def gather_over(shard, name, dim):
+    size = lax.axis_size(name)
+    blocks = jnp.stack([shard for _ in range(size)])
+    blocks = lax.all_to_all(blocks, name, split_axis=0, concat_axis=0)
+    return jnp.concatenate(blocks, axis=dim)
+
+
 def layer_norm(video):
     values = video.astype(jnp.float32)
     center = values - jnp.mean(values, axis=-1, keepdims=True)
@@ -16,7 +23,7 @@
 
 
 def negative_rows(neg_kv):
-    return lax.all_gather(neg_kv, "bag", axis=0, tiled=True)
+    return gather_over(neg_kv, "bag", 0)
 
 
 def attend(query_rms, keys, values, length):

time: 259 us -> 200 us (0.77)
  waiting for transfers between devices: 131 us -> 70.1 us
  local copies, waits for them, and re-layouts: 41.3 us -> 29.2 us
  starting transfers between devices: 0.04 us -> 12.1 us
    all_gather x1 -> x0, waiting for transfers between devices: 55.3 us -> none  [negative_rows(): return lax.all_gather(neg_kv, 'bag', axis=0, tiled=True)]
    all_gather x1, waiting for transfers between devices: 74 us -> 20.5 us  [body(): gathered = lax.all_gather(w_query, 'bag', axis=0, tiled=True)]
    all_to_all x0 -> x1, waiting for transfers between devices: none -> 48.9 us  [gather_over(): blocks = lax.all_to_all(blocks, name, split_axis=0, concat_axis=0)]
    all_to_all x0 -> x1, starting transfers between devices: none -> 12.1 us  [gather_over(): blocks = lax.all_to_all(blocks, name, split_axis=0, concat_axis=0)]
    slice x2 -> x3, local copies, waits for them, and re-layouts: 11.4 us -> 3.14 us  [body(): uncond = attend(query_rms, negative[:, 0], negative[:, 1], neg_len[0])]
    unnamed x6 -> x10, local copies, waits for them, and re-layouts: 12.4 us -> 7.11 us
  transfers between devices with their start and end apart: 2 -> 2, of which waited for: 2 -> 2; matrix products, arithmetic and copies ran while one was open for 17% -> 15% of each run, Pallas kernels for 0% -> 0%
where the time goes in v1:
time: 200 us; the launch traced here: 197 us
  waiting for transfers between devices  70.1 us (35%)
  matrix products  48 us (24%)
  local copies, waits for them, and re-layouts  29.2 us (15%)
  between operations  14.8 us (7%)
  other arithmetic  12.4 us (6%)
  starting transfers between devices  12.1 us (6%)
  blocking collectives  10.6 us (5%)
    all_to_all x1, waiting for transfers between devices, gather_over(): blocks = lax.all_to_all(blocks, name, split_axis=0, concat_axis=0)  48.9 us
    sub x2, matrix products, attend(): weights = jnp.where(live, jnp.exp(scores - top), jnp.float32(0.0))  20.9 us
    all_gather x1, waiting for transfers between devices, body(): gathered = lax.all_gather(w_query, 'bag', axis=0, tiled=True)  20.5 us
    dot_general x1, matrix products, body(): query = jnp.dot(normed, gathered, preferred_element_type=jnp.float32)  14 us
    dot_general x2, matrix products, attend(): jnp.einsum('hts,shd->thd', weights, v_heads, preferred_element_type=jnp.f...  13.1 us
    all_to_all x1, starting transfers between devices, gather_over(): blocks = lax.all_to_all(blocks, name, split_axis=0, concat_axis=0)  12.1 us
    psum x1, blocking collectives, body(): squares = lax.psum(jnp.sum(query * query, axis=1), 'seq')  10.6 us
    slice x2, local copies, waits for them, and re-layouts, body(): cond = attend(query_rms, cond_kv[0, :, 0], cond_kv[0, :, 1], prompt_len[0])  9.31 us
  transfers between devices with their start and end apart: 2, of which 2 were waited for; matrix products, arithmetic and copies ran while one was open for 15% of the time, Pallas kernels for 0%

profile of v1, /device:TPU:32, one launch (start us, length us, event | category | flops | bytes accessed | tf_op | source)
XLA Modules:
  0.0 197.2 jit_solution(7601800100922266700)
XLA Ops:
  6.5 0.0 all-gather.2.cloned.1.call-start
  6.5 0.7 all-gather.2.cloned.1.call-update
  7.3 0.8 copy.32
  8.0 1.6 stack.2
  9.7 0.0 copy-start
  9.7 12.1 %all-to-all-start = ((bf16[64,8,2,1280]{3,1,2,0:T(8,128)(2,1)}), bf16[64,8,2,1280]{3,1,2,0:T(8,128)(2,1)}, u32[]{:S(2)}, u32[]{:S(2)}) async-start(bf16[64,8,2,1280]{3,1,2,0:T(8,128)(2,1)} %stack.2), calls=%async_computation | async-start | bytes 5242880 | tf_op jit(solution)/shard_map/all_to_all | solution.py:14
  21.8 0.0 copy-done
  21.8 5.4 %fusion.28 = (bf16[1,512,1,1280]{3,2,1,0:T(2,128)(2,1)}, bf16[1,512,1,1280]{3,2,1,0:T(2,128)(2,1)}) fusion(bf16[1,512,2,1280]{3,2,1,0:T(2,128)(2,1)S(1)} %copy-done), kind=kLoop, calls=%fused_computation.42 | loop fusion | bytes 5242880 | tf_op jit(solution)/shard_map/slice | solution.py:55
  27.2 0.0 copy-start.1
  27.2 6.3 %copy.53 = bf16[1,512,1,1280]{1,3,2,0:T(8,128)(2,1)} copy(bf16[1,512,1,1280]{3,2,1,0:T(2,128)(2,1)} %get-tuple-element.5) | data formatting | bytes 2621440
  34.1 0.0 copy-done.1
  34.2 3.9 %copy.42 = bf16[1,512,1,1280]{1,3,2,0:T(8,128)(2,1)} copy(bf16[1,512,1,1280]{3,2,1,0:T(2,128)(2,1)S(1)} %copy-done.1) | data formatting | bytes 2621440 | tf_op jit(solution)/shard_map/slice | solution.py:55
  38.7 3.3 %convert_reduce_fusion = f32[512]{0:T(512)S(1)} fusion(bf16[512,5120]{1,0:T(8,128)(2,1)} %param.6), kind=kLoop, calls=%fused_computation.3 | loop fusion | flops 5242368 | bytes 5244928 | tf_op jit(solution)/shard_map/reduce_sum | solution.py:20
  42.0 4.0 %fusion.4 = f32[512]{0:T(512)S(1)} fusion(bf16[512,5120]{1,0:T(8,128)(2,1)} %param.6, f32[512]{0:T(512)S(1)} %broadcast_multiply_fusion), kind=kLoop, calls=%fused_computation.6 | loop fusion | flops 10485248 | bytes 5246976 | tf_op jit(solution)/shard_map/reduce_sum | solution.py:21
  46.0 48.9 %all-to-all-done = bf16[64,8,2,1280]{3,1,2,0:T(8,128)(2,1)} async-done(((bf16[64,8,2,1280]{3,1,2,0:T(8,128)(2,1)}), bf16[64,8,2,1280]{3,1,2,0:T(8,128)(2,1)}, u32[]{:S(2)}, u32[]{:S(2)}) %all-to-all-start) | async-done | bytes 2621472 | tf_op jit(solution)/shard_map/all_to_all | solution.py:14
  94.9 2.0 copy.55
  96.9 0.2 fusion.29
  97.1 1.5 copy.34
  98.6 1.5 copy.37
  100.0 20.5 %all-gather.2.cloned.1.call-done = bf16[5120,1280]{1,0:T(8,128)(2,1)} async-done(((bf16[80,1280]{1,0:T(8,128)(2,1)}), bf16[5120,1280]{1,0:T(8,128)(2,1)}) %all-gather.2.cloned.1.call-update) | async-done | bytes 13107216 | tf_op jit(solution)/shard_map/all_gather | solution.py:50
  120.5 14.0 %multiply_reduce_fusion = (f32[512]{0:T(512)S(1)}, f32[512,1280]{1,0:T(8,128)}) fusion(bf16[5120,1280]{1,0:T(8,128)(2,1)} %all-gather.2.cloned.1.call-done, bf16[512,5120]{1,0:T(8,128)(2,1)} %param.6, f32[512]{0:T(512)S(1)} %add_rsqrt_fusion.1, f32[512]{0:T(512)S(1)} %broadcast_multiply_fusion), kind=kOutput, calls=%fused_computation.30 | convolution fusion | flops 6722682368 | bytes 20977664 | tf_op jit(solution)/shard_map/dot_general | solution.py:51
  134.5 10.6 %psum.7 = f32[512]{0:T(512)S(1)} all-reduce(f32[512]{0:T(512)S(1)} %get-tuple-element.9), channel_id=1, replica_groups=mesh['bag'=64,'seq'=4] {'seq'}, use_global_device_ids=true, to_apply=%region_3.0 | all-reduce | flops 512 | bytes 4096 | tf_op jit(solution)/shard_map/psum | solution.py:52
  145.2 1.9 multiply_convert_fusion
  147.1 0.7 copy.31
  147.8 0.0 copy-start.2
  147.8 0.0 copy-start.3
  147.8 10.5 %fusion.31 = (f32[10,512]{1,0:T(8,128)S(1)}, f32[10,512,512]{1,2,0:T(8,128)}) fusion(pred[512]{0:T(512)(128)(4,1)S(1)} %iota_compare_fusion, bf16[512,10,128]{0,2,1:T(8,128)(2,1)S(1)} %bitcast.34, bf16[512,10,128]{0,2,1:T(8,128)(2,1)} %bitcast.36), kind=kOutput, calls=%fused_computation.45 | convolution fusion | flops 684196352 | bytes 13128192 | tf_op jit(solution)/shard_map/sub | solution.py:42
  158.3 0.0 copy-done.2
  158.3 0.0 copy-done.3
  158.3 6.4 %fusion.19 = f32[10,512,128]{1,2,0:T(8,128)} fusion(bf16[512,10,128]{0,2,1:T(8,128)(2,1)S(1)} %bitcast.37, f32[10,512,512]{1,2,0:T(8,128)} %get-tuple-element.14, f32[10,512]{1,0:T(8,128)S(1)} %get-tuple-element.13), kind=kOutput, calls=%fused_computation.26 | convolution fusion | flops 676331520 | bytes 14438400 | tf_op jit(solution)/shard_map/hts,shd->thd/dot_general | solution.py:44
  164.7 2.1 %copy.44 = f32[512,1280]{1,0:T(8,128)S(1)} copy(f32[512,1280]{0,1:T(8,128)} %bitcast.30) | data formatting | bytes 5242880 | tf_op jit(solution)/shard_map/reshape | solution.py:45
  166.8 10.4 %fusion.30 = (f32[10,512]{1,0:T(8,128)S(1)}, f32[10,512,512]{1,2,0:T(8,128)}) fusion(pred[512]{0:T(512)(128)(4,1)S(1)} %iota_compare_fusion.1, bf16[512,10,128]{0,2,1:T(8,128)(2,1)} %bitcast.35, bf16[512,10,128]{0,2,1:T(8,128)(2,1)} %bitcast.33), kind=kOutput, calls=%fused_computation.44 | convolution fusion | flops 684196352 | bytes 13128192 | tf_op jit(solution)/shard_map/sub | solution.py:42
  177.2 6.8 %fusion.18 = f32[10,512,128]{1,2,0:T(8,128)} fusion(bf16[512,10,128]{0,2,1:T(8,128)(2,1)} %bitcast.32, f32[10,512,512]{1,2,0:T(8,128)} %get-tuple-element.12, f32[10,512]{1,0:T(8,128)S(1)} %get-tuple-element.11), kind=kOutput, calls=%fused_computation.25 | convolution fusion | flops 676331520 | bytes 14438400 | tf_op jit(solution)/shard_map/hts,shd->thd/dot_general | solution.py:44
  184.0 3.2 %copy.46 = f32[512,1280]{1,0:T(8,128)} copy(f32[512,1280]{0,1:T(8,128)} %bitcast.31) | data formatting | bytes 5242880 | tf_op jit(solution)/shard_map/reshape | solution.py:45
  187.2 3.1 %add_convert_fusion = bf16[512,1280]{1,0:T(8,128)(2,1)} fusion(f32[512,1280]{1,0:T(8,128)} %copy.46, f32[512,1280]{1,0:T(8,128)S(1)} %copy.44), kind=kLoop, calls=%fused_computation.28 | loop fusion | flops 2621440 | bytes 6553600 | tf_op jit(solution)/shard_map/convert_element_type | solution.py:57
  (5 shorter events, 0.0 us)
Async XLA Ops:
  6.5 114.0 %all-gather.2.cloned.1.call-start = ((), (), s32[]{:S(2)}) async-start(), calls=%async_computation.1 | async-start | bytes 13312000 | tf_op jit(solution)/shard_map/all_gather | solution.py:50
  9.7 12.1 %copy-start = (bf16[1,512,2,1280]{3,2,1,0:T(2,128)(2,1)S(1)}, bf16[1,512,2,1280]{3,2,1,0:T(2,128)(2,1)}, u32[]{:S(2)}) copy-start(bf16[1,512,2,1280]{3,2,1,0:T(2,128)(2,1)} %param.8) | copy-start | bytes 7864324
  9.7 85.2 %all-to-all-start = ((bf16[64,8,2,1280]{3,1,2,0:T(8,128)(2,1)}), bf16[64,8,2,1280]{3,1,2,0:T(8,128)(2,1)}, u32[]{:S(2)}, u32[]{:S(2)}) async-start(bf16[64,8,2,1280]{3,1,2,0:T(8,128)(2,1)} %stack.2), calls=%async_computation | async-start | bytes 5242880 | tf_op jit(solution)/shard_map/all_to_all | solution.py:14
  27.2 7.0 %copy-start.1 = (bf16[1,512,1,1280]{3,2,1,0:T(2,128)(2,1)S(1)}, bf16[1,512,1,1280]{3,2,1,0:T(2,128)(2,1)}, u32[]{:S(2)}) copy-start(bf16[1,512,1,1280]{3,2,1,0:T(2,128)(2,1)} %get-tuple-element.6) | copy-start | bytes 3932164
  147.8 10.5 %copy-start.2 = (bf16[512,1280]{0,1:T(8,128)(2,1)}, bf16[512,1280]{0,1:T(8,128)(2,1)S(1)}, u32[]{:S(2)}) copy-start(bf16[512,1280]{0,1:T(8,128)(2,1)S(1)} %copy.31) | copy-start | bytes 3932164
  147.8 10.5 %copy-start.3 = (bf16[1,512,1,1280]{1,3,2,0:T(8,128)(2,1)S(1)}, bf16[1,512,1,1280]{1,3,2,0:T(8,128)(2,1)}, u32[]{:S(2)}) copy-start(bf16[1,512,1,1280]{1,3,2,0:T(8,128)(2,1)} %copy.42) | copy-start | bytes 3932164
Sparse Core Ops, SparseCore 0:
  10.1 110.4 all-gather.1
